TPU v7x, 32 devices: a whole 2x2x4 slice. The times are simulated.
32 devices in a mesh: blk: 8 (over y, x, core), rep: 4 (over z).
Axes of the slice: x: 2, y: 2, z: 4, core: 2. Of those that a mesh axis runs over, the one named last changes fastest.
Arguments:
- coords: float32 [3, 1200, 2048], P(None, 'rep', 'blk'), may hold values from -40 to 40
- frame_count: int32 [8], P('blk'), may hold values from 64 to 256, as said below
Outputs:
- deviation_behind: float32 [3, 2048, 256], P(None, ('blk', 'rep'))
- deviation_ahead: float32 [3, 2048, 256], P(None, ('blk', 'rep'))
Inputs may be any that keep to these rules, and one draw needn't show every extreme that they name: `frame_count`: at least one block is full and at least one holds exactly 64 frames.
All inputs are finite; a program needn't handle non-finite values.
Results may differ from a plain program's by a relative error of at most 0.0003.
Values sent between devices are 32-bit elements; how exact they have to be, the bound alone decides.
A program may use at most 64 MiB of HBM per device.

v0:
```python
import jax
import jax.numpy as jnp
from jax import lax
from jax.sharding import PartitionSpec as P

NATOM = 1200
ROUNDS = 3
NEWTON = 4


def from_behind(block, axis, distance):
    devices = range(lax.axis_size(axis))
    route = [((i - distance) % len(devices), i) for i in devices]
    return lax.ppermute(block, axis, route)


def pair_minor(upper, lower, left, right):
    return upper[left] * lower[right] - upper[right] * lower[left]


def deviation(covariance, own_sq, other_sq):
    m = [[covariance[first, :, second, :] for second in range(3)] for first in range(3)]
    keyed = [
        [m[0][0] + m[1][1] + m[2][2], m[1][2] - m[2][1], m[2][0] - m[0][2], m[0][1] - m[1][0]],
        [m[1][2] - m[2][1], m[0][0] - m[1][1] - m[2][2], m[0][1] + m[1][0], m[2][0] + m[0][2]],
        [m[2][0] - m[0][2], m[0][1] + m[1][0], -m[0][0] + m[1][1] - m[2][2], m[1][2] + m[2][1]],
        [m[0][1] - m[1][0], m[2][0] + m[0][2], m[1][2] + m[2][1], -m[0][0] - m[1][1] + m[2][2]],
    ]
    top_one, top_two, low_one, low_two = keyed
    det_key = (
        pair_minor(top_one, top_two, 0, 1) * pair_minor(low_one, low_two, 2, 3)
        - pair_minor(top_one, top_two, 0, 2) * pair_minor(low_one, low_two, 1, 3)
        + pair_minor(top_one, top_two, 0, 3) * pair_minor(low_one, low_two, 1, 2)
        + pair_minor(top_one, top_two, 1, 2) * pair_minor(low_one, low_two, 0, 3)
        - pair_minor(top_one, top_two, 1, 3) * pair_minor(low_one, low_two, 0, 2)
        + pair_minor(top_one, top_two, 2, 3) * pair_minor(low_one, low_two, 0, 1)
    )
    det_three = (
        m[0][0] * (m[1][1] * m[2][2] - m[1][2] * m[2][1])
        - m[0][1] * (m[1][0] * m[2][2] - m[1][2] * m[2][0])
        + m[0][2] * (m[1][0] * m[2][1] - m[1][1] * m[2][0])
    )
    square_sum = m[0][0] * m[0][0]
    for first in range(3):
        for second in range(3):
            if first + second > 0:
                square_sum = square_sum + m[first][second] * m[first][second]
    second_coef = -2.0 * square_sum
    first_coef = -8.0 * det_three
    total = own_sq[:, None] + other_sq[None, :]
    largest = 0.5 * total
    for newton_step in range(NEWTON):
        squared = largest * largest
        polynomial = squared * squared + second_coef * squared + first_coef * largest + det_key
        derivative = 4.0 * squared * largest + 2.0 * second_coef * largest + first_coef
        largest = largest - polynomial / derivative
    return total - 2.0 * largest


def shards(coords, frame_count):
    block_rows = coords.shape[2]
    rep_count = lax.axis_size("rep")
    quarter = block_rows // rep_count
    start = lax.axis_index("rep") * quarter
    atom_sums = lax.psum(jnp.sum(coords, axis=1), "rep")
    centroid = atom_sums / NATOM
    centered = coords - centroid[:, None, :]
    self_sq = lax.psum(jnp.sum(centered * centered, axis=(0, 1)), "rep") / NATOM
    block_count = frame_count.astype(jnp.float32)
    columns = jnp.arange(block_rows, dtype=jnp.float32)
    own_valid = columns < block_count[0]
    whole_atoms = lax.all_gather(centered, "rep", axis=1, tiled=True)
    mine = (
        lax.dynamic_slice_in_dim(whole_atoms, start, quarter, 2),
        lax.dynamic_slice_in_dim(self_sq, start, quarter),
        block_count,
    )
    partner_columns = start.astype(jnp.float32) + jnp.arange(quarter, dtype=jnp.float32)
    held = mine
    behind_list = []
    ahead_list = []
    for distance in range(1, ROUNDS + 1):
        held = from_behind((mine[0], mine[1], mine[2]), "blk", distance)
        partner_coords, partner_sq, partner_count = held
        other_valid = partner_columns < partner_count[0]
        covariance = (
            lax.dot_general(
                whole_atoms,
                partner_coords,
                (((1,), (1,)), ((), ())),
                precision=lax.Precision.HIGHEST,
            )
            / NATOM
        )
        mask = own_valid[:, None] & other_valid[None, :]
        square = jnp.where(mask, deviation(covariance, self_sq, partner_sq), 0.0)
        behind = lax.all_to_all(square, "rep", split_axis=0, concat_axis=1, tiled=True)
        ahead = from_behind(square, "blk", -distance).T
        behind_list.append(behind)
        ahead_list.append(ahead)
    return (jnp.stack(behind_list, 0), jnp.stack(ahead_list, 0))


def solution(mesh):
    in_specs = (P(None, "rep", "blk"), P("blk"))
    out_specs = (P(None, ("blk", "rep"), None), P(None, ("blk", "rep"), None))
    return jax.shard_map(shards, mesh=mesh, in_specs=in_specs, out_specs=out_specs, check_vma=False)
```

profile of v0, /device:TPU:0, one launch (start us, length us, event | category | flops | bytes accessed | tf_op | source)
XLA Modules:
  0.0 228.2 jit_solution(13288192395959160833)
XLA Ops:
  7.2 1.3 reduce_sum.18
  8.5 13.5 %psum.14 = f32[3,256]{1,0:T(4,128)S(1)} all-reduce(f32[3,256]{1,0:T(4,128)S(1)} %reduce_sum.18), channel_id=1, replica_groups=mesh['blk'=8,'rep'=4] {'rep'}, use_global_device_ids=true, to_apply=%region_1.0 | all-reduce | flops 768 | bytes 6144 | tf_op jit(solution)/shard_map/psum | solution.py:65
  22.0 3.0 %multiply_reduce_fusion = (f32[256]{0:T(256)S(1)}, f32[3,300,256]{2,0,1:T(4,128)}) fusion(f32[3,256]{1,0:T(4,128)S(1)} %broadcast_multiply_fusion, f32[3,300,256]{2,1,0:T(8,128)} %param.2), kind=kLoop, calls=%fused_computation.10 | loop fusion | flops 690944 | bytes 1847296 | tf_op jit(solution)/shard_map/reduce_sum | solution.py:68
  24.9 91.0 %all-gather.2.cloned.1.call-done = f32[3,1200,256]{2,0,1:T(4,128)} async-done(((f32[3,300,256]{2,0,1:T(4,128)}), f32[3,1200,256]{2,0,1:T(4,128)}) %all-gather.2.cloned.1.call-update) | async-done | bytes 3686416 | tf_op jit(solution)/shard_map/all_gather | solution.py:72
  115.9 2.7 %constant_dynamic-slice_fusion = f32[3,1200,64]{2,0,1:T(4,128)S(1)} fusion(f32[3,1200,256]{2,0,1:T(4,128)} %all-gather.2.cloned.1.call-done, s32[]{:T(128)S(6)} %select_n.23), kind=kLoop, calls=%fused_computation.429 | loop fusion | bytes 1843204 | tf_op jit(solution)/shard_map/dynamic_slice | solution.py:74
  118.6 1.4 copy.196
  120.1 8.8 %psum.15 = f32[256]{0:T(256)S(1)} all-reduce(f32[256]{0:T(256)S(1)} %get-tuple-element.2), channel_id=1, replica_groups=mesh['blk'=8,'rep'=4] {'rep'}, use_global_device_ids=true, to_apply=%region_3.0 | all-reduce | flops 256 | bytes 2048 | tf_op jit(solution)/shard_map/psum | solution.py:68
  129.1 1.7 collective-permute-start.4
  131.4 2.3 collective-permute-start
  133.7 1.5 collective-permute-start.5
  135.3 0.2 collective-permute-done
  135.5 21.0 %collective-permute-start.3 = (f32[1]{0:T(128)}, f32[1]{0:T(128)}, u32[]{:S(2)}, u32[]{:S(2)}) collective-permute-start(f32[1]{0:T(128)} %convert_element_type.6), channel_id=1, source_target_pairs={{24,0},{28,4},{0,8},{4,12},{8,16},{12,20},{16,24},{20,28},{25,1},{... | collective-permute-start | bytes 20 | tf_op jit(solution)/shard_map/ppermute | solution.py:14
  156.5 0.6 fusion.278
  157.1 1.4 collective-permute-done.3
  158.5 1.3 collective-permute-start.6
  159.8 0.6 fusion.277
  160.4 1.2 collective-permute-done.6
  161.6 0.6 fusion.276
  162.2 0.9 collective-permute-start.8
  163.1 5.7 %fusion.6 = f32[3,256,3,64]{1,3,2,0:T(8,128)S(1)} fusion(f32[3,1200,256,1]{2,0,1,3:T(4,128)} %bitcast.1114, f32[3,1200,64]{1,2,0:T(8,128)S(1)} %collective-permute-done.2), kind=kOutput, calls=%fused_computation.6 | convolution fusion | flops 2123513856 | bytes 5197824 | tf_op jit(solution)/shard_map/dot_general | solution.py:87
  168.8 1.0 fusion.118
  169.8 1.9 collective-permute-start.9
  171.7 3.3 %fusion.9 = f32[3,256,3,64]{1,3,2,0:T(8,128)S(1)} fusion(f32[3,1200,256,1]{2,0,1,3:T(4,128)S(1)} %bitcast.1115, f32[3,1200,64]{1,2,0:T(8,128)S(1)} %collective-permute-done.5), kind=kOutput, calls=%fused_computation.7 | convolution fusion | flops 2123513856 | bytes 5197824 | tf_op jit(solution)/shard_map/dot_general | solution.py:87
  175.1 1.0 fusion.123
  176.1 0.5 collective-permute-start.10
  176.7 9.6 %collective-permute-done.8 = f32[3,1200,64]{1,2,0:T(8,128)S(1)} collective-permute-done((f32[3,1200,64]{1,2,0:T(8,128)S(1)}, f32[3,1200,64]{1,2,0:T(8,128)S(1)}, u32[]{:S(2)}, u32[]{:S(2)}) %collective-permute-start.8) | collective-permute-done | bytes 921632 | tf_op jit(solution)/shard_map/ppermute | solution.py:14
  186.3 3.4 %fusion.12 = f32[3,256,3,64]{1,3,2,0:T(8,128)S(1)} fusion(f32[3,1200,256,1]{2,0,1,3:T(4,128)S(1)} %bitcast.1116, f32[3,1200,64]{1,2,0:T(8,128)S(1)} %collective-permute-done.8), kind=kOutput, calls=%fused_computation.8 | convolution fusion | flops 2123513856 | bytes 5197824 | tf_op jit(solution)/shard_map/dot_general | solution.py:87
  189.7 0.4 fusion.128
  191.2 0.7 fusion.284
  191.9 0.8 reshape.132
  192.7 3.3 %all-to-all-start = ((f32[4,1,4096]{2,1,0:T(1,128)}), f32[4,1,4096]{2,1,0:T(1,128)S(1)}, u32[]{:S(2)}, u32[]{:S(2)}) async-start(f32[4,1,4096]{2,1,0:T(1,128)} %reshape.132), calls=%async_computation | async-start | bytes 131072 | tf_op jit(solution)/shard_map/all_to_all | solution.py:97
  197.0 0.7 fusion.283
  197.7 0.8 reshape.130
  199.5 2.2 all-to-all-done
  201.7 3.3 %all-to-all-start.1 = ((f32[4,1,4096]{2,1,0:T(1,128)}), f32[4,1,4096]{2,1,0:T(1,128)S(1)}, u32[]{:S(2)}, u32[]{:S(2)}) async-start(f32[4,1,4096]{2,1,0:T(1,128)} %reshape.130), calls=%async_computation.1 | async-start | bytes 131072 | tf_op jit(solution)/shard_map/all_to_all | solution.py:97
  205.0 0.7 fusion.282
  205.7 0.8 reshape.128
  206.5 4.2 %all-to-all-done.1 = f32[4,1,4096]{2,1,0:T(1,128)S(1)} async-done(((f32[4,1,4096]{2,1,0:T(1,128)}), f32[4,1,4096]{2,1,0:T(1,128)S(1)}, u32[]{:S(2)}, u32[]{:S(2)}) %all-to-all-start.1) | async-done | bytes 65568 | tf_op jit(solution)/shard_map/all_to_all | solution.py:97
  210.7 3.3 %all-to-all-start.2 = ((f32[4,1,4096]{2,1,0:T(1,128)}), f32[4,1,4096]{2,1,0:T(1,128)S(1)}, u32[]{:S(2)}, u32[]{:S(2)}) async-start(f32[4,1,4096]{2,1,0:T(1,128)} %reshape.128), calls=%async_computation.2 | async-start | bytes 131072 | tf_op jit(solution)/shard_map/all_to_all | solution.py:97
  214.0 1.6 pad_maximum_fusion.1
  215.6 0.5 broadcast.209
  216.1 0.7 reduce.2
  216.8 0.1 reshape.133
  217.0 0.7 reduce.1
  218.0 1.7 all-to-all-done.2
  219.7 0.7 reduce
  220.4 0.1 reshape.129
  220.6 0.7 pad_maximum_fusion
  (56 shorter events, 3.9 us)
Async XLA Ops:
  7.2 108.8 %all-gather.2.cloned.1.call-start = ((), (), s32[]{:S(2)}) async-start(), calls=%async_computation.3 | async-start | bytes 6144000 | tf_op jit(solution)/shard_map/all_gather | solution.py:72
  120.1 42.1 %collective-permute-start.2 = (f32[3,1200,64]{1,2,0:T(8,128)S(1)}, f32[3,1200,64]{1,2,0:T(8,128)S(1)}, u32[]{:S(2)}, u32[]{:S(2)}) collective-permute-start(f32[3,1200,64]{1,2,0:T(8,128)S(1)} %copy.196), channel_id=1, source_target_pairs={{28,0},{0,4},{4,8},{8,12},{12,16},{16,20},{20,24},{24,28},{29,1},{... | collective-permute-start | bytes 2764808 | tf_op jit(solution)/shard_map/ppermute | solution.py:14
  129.1 39.7 %collective-permute-start.1 = (f32[64]{0:T(128)S(1)}, f32[64]{0:T(128)S(1)}, u32[]{:S(2)}, u32[]{:S(2)}) collective-permute-start(f32[64]{0:T(128)S(1)} %dynamic_slice.6), channel_id=1, source_target_pairs={{28,0},{0,4},{4,8},{8,12},{12,16},{16,20},{20,24},{24,28},{29,1},{... | collective-permute-start | bytes 776 | tf_op jit(solution)/shard_map/ppermute | solution.py:14
  129.1 46.0 %collective-permute-start.4 = (f32[64]{0:T(128)S(1)}, f32[64]{0:T(128)S(1)}, u32[]{:S(2)}, u32[]{:S(2)}) collective-permute-start(f32[64]{0:T(128)S(1)} %dynamic_slice.6), channel_id=1, source_target_pairs={{24,0},{28,4},{0,8},{4,12},{8,16},{12,20},{16,24},{20,28},{25,1},{... | collective-permute-start | bytes 776 | tf_op jit(solution)/shard_map/ppermute | solution.py:14
  131.4 4.0 %collective-permute-start = (f32[1]{0:T(128)}, f32[1]{0:T(128)}, u32[]{:S(2)}, u32[]{:S(2)}) collective-permute-start(f32[1]{0:T(128)} %convert_element_type.6), channel_id=1, source_target_pairs={{28,0},{0,4},{4,8},{8,12},{12,16},{16,20},{20,24},{24,28},{29,1},{... | collective-permute-start | bytes 20 | tf_op jit(solution)/shard_map/ppermute | solution.py:14
  133.7 38.0 %collective-permute-start.5 = (f32[3,1200,64]{1,2,0:T(8,128)S(1)}, f32[3,1200,64]{1,2,0:T(8,128)S(1)}, u32[]{:S(2)}, u32[]{:S(2)}) collective-permute-start(f32[3,1200,64]{1,2,0:T(8,128)S(1)} %copy.196), channel_id=1, source_target_pairs={{24,0},{28,4},{0,8},{4,12},{8,16},{12,20},{16,24},{20,28},{25,1},{... | collective-permute-start | bytes 2764808 | tf_op jit(solution)/shard_map/ppermute | solution.py:14
  135.3 36.4 %copy-start = (f32[3,1200,256]{2,0,1:T(4,128)S(1)}, f32[3,1200,256]{2,0,1:T(4,128)}, u32[]{:S(2)}) copy-start(f32[3,1200,256]{2,0,1:T(4,128)} %all-gather.2.cloned.1.call-done) | copy-start | bytes 11059204
  135.5 23.0 %collective-permute-start.3 = (f32[1]{0:T(128)}, f32[1]{0:T(128)}, u32[]{:S(2)}, u32[]{:S(2)}) collective-permute-start(f32[1]{0:T(128)} %convert_element_type.6), channel_id=1, source_target_pairs={{24,0},{28,4},{0,8},{4,12},{8,16},{12,20},{16,24},{20,28},{25,1},{... | collective-permute-start | bytes 20 | tf_op jit(solution)/shard_map/ppermute | solution.py:14
  158.5 3.1 %collective-permute-start.6 = (f32[1]{0:T(128)}, f32[1]{0:T(128)}, u32[]{:S(2)}, u32[]{:S(2)}) collective-permute-start(f32[1]{0:T(128)} %convert_element_type.6), channel_id=1, source_target_pairs={{20,0},{24,4},{28,8},{0,12},{4,16},{8,20},{12,24},{16,28},{21,1},{... | collective-permute-start | bytes 20 | tf_op jit(solution)/shard_map/ppermute | solution.py:14
  161.6 28.1 %collective-permute-start.7 = (f32[64]{0:T(128)S(1)}, f32[64]{0:T(128)S(1)}, u32[]{:S(2)}, u32[]{:S(2)}) collective-permute-start(f32[64]{0:T(128)S(1)} %dynamic_slice.6), channel_id=1, source_target_pairs={{20,0},{24,4},{28,8},{0,12},{4,16},{8,20},{12,24},{16,28},{21,1},{... | collective-permute-start | bytes 776 | tf_op jit(solution)/shard_map/ppermute | solution.py:14
  162.2 24.1 %collective-permute-start.8 = (f32[3,1200,64]{1,2,0:T(8,128)S(1)}, f32[3,1200,64]{1,2,0:T(8,128)S(1)}, u32[]{:S(2)}, u32[]{:S(2)}) collective-permute-start(f32[3,1200,64]{1,2,0:T(8,128)S(1)} %copy.196), channel_id=1, source_target_pairs={{20,0},{24,4},{28,8},{0,12},{4,16},{8,20},{12,24},{16,28},{21,1},{... | collective-permute-start | bytes 2764808 | tf_op jit(solution)/shard_map/ppermute | solution.py:14
  169.8 44.2 %collective-permute-start.9 = (f32[256,64]{0,1:T(8,128)}, f32[256,64]{0,1:T(8,128)}, u32[]{:S(2)}, u32[]{:S(2)}) collective-permute-start(f32[256,64]{0,1:T(8,128)} %fusion.118), channel_id=1, source_target_pairs={{4,0},{8,4},{12,8},{16,12},{20,16},{24,20},{28,24},{0,28},{5,1},{9... | collective-permute-start | bytes 196616 | tf_op jit(solution)/shard_map/ppermute | solution.py:14
  176.1 38.0 %collective-permute-start.10 = (f32[256,64]{0,1:T(8,128)}, f32[256,64]{0,1:T(8,128)}, u32[]{:S(2)}, u32[]{:S(2)}) collective-permute-start(f32[256,64]{0,1:T(8,128)} %fusion.123), channel_id=1, source_target_pairs={{8,0},{12,4},{16,8},{20,12},{24,16},{28,20},{0,24},{4,28},{9,1},{1... | collective-permute-start | bytes 196616 | tf_op jit(solution)/shard_map/ppermute | solution.py:14
  190.1 23.9 %collective-permute-start.11 = (f32[256,64]{0,1:T(8,128)S(1)}, f32[256,64]{0,1:T(8,128)S(1)}, u32[]{:S(2)}, u32[]{:S(2)}) collective-permute-start(f32[256,64]{0,1:T(8,128)S(1)} %fusion.128), channel_id=1, source_target_pairs={{12,0},{16,4},{20,8},{24,12},{28,16},{0,20},{4,24},{8,28},{13,1},{... | collective-permute-start | bytes 196616 | tf_op jit(solution)/shard_map/ppermute | solution.py:14
  192.7 9.0 %all-to-all-start = ((f32[4,1,4096]{2,1,0:T(1,128)}), f32[4,1,4096]{2,1,0:T(1,128)S(1)}, u32[]{:S(2)}, u32[]{:S(2)}) async-start(f32[4,1,4096]{2,1,0:T(1,128)} %reshape.132), calls=%async_computation | async-start | bytes 131072 | tf_op jit(solution)/shard_map/all_to_all | solution.py:97
  201.7 9.0 %all-to-all-start.1 = ((f32[4,1,4096]{2,1,0:T(1,128)}), f32[4,1,4096]{2,1,0:T(1,128)S(1)}, u32[]{:S(2)}, u32[]{:S(2)}) async-start(f32[4,1,4096]{2,1,0:T(1,128)} %reshape.130), calls=%async_computation.1 | async-start | bytes 131072 | tf_op jit(solution)/shard_map/all_to_all | solution.py:97
  210.7 9.0 %all-to-all-start.2 = ((f32[4,1,4096]{2,1,0:T(1,128)}), f32[4,1,4096]{2,1,0:T(1,128)S(1)}, u32[]{:S(2)}, u32[]{:S(2)}) async-start(f32[4,1,4096]{2,1,0:T(1,128)} %reshape.128), calls=%async_computation.2 | async-start | bytes 131072 | tf_op jit(solution)/shard_map/all_to_all | solution.py:97
Sparse Core Ops, SparseCore 0:
  25.1 90.8 all-gather.1
where the time goes:
time: 229 us; the launch traced here: 228 us
  waiting for transfers between devices  112 us (49%)
  starting transfers between devices  41 us (18%)
  blocking collectives  22.3 us (10%)
  between operations  15 us (7%)
  other arithmetic  14.9 us (7%)
  matrix products  12.4 us (5%)
  local copies, waits for them, and re-layouts  10.9 us (5%)
    all_gather x1, waiting for transfers between devices, shards(): whole_atoms = lax.all_gather(centered, 'rep', axis=1, tiled=True)  91 us
    ppermute x12, starting transfers between devices, from_behind(): return lax.ppermute(block, axis, route)  31.1 us
    psum x1, blocking collectives, shards(): atom_sums = lax.psum(jnp.sum(coords, axis=1), 'rep')  13.5 us
    ppermute x12, waiting for transfers between devices, from_behind(): return lax.ppermute(block, axis, route)  12.5 us
    dot_general x3, matrix products, shards(): lax.dot_general(whole_atoms, partner_coords, (((1,), (1,)), ((), ())), pr...  12.4 us
    all_to_all x3, starting transfers between devices, shards(): lax.all_to_all(square, 'rep', split_axis=0, concat_axis=1, tiled=True)  9.86 us
    psum x1, blocking collectives, shards(): self_sq = lax.psum(jnp.sum(centered * centered, axis=(0, 1)), 'rep') / NATOM  8.85 us
    all_to_all x3, waiting for transfers between devices, shards(): lax.all_to_all(square, 'rep', split_axis=0, concat_axis=1, tiled=True)  8.13 us
  transfers between devices with their start and end apart: 16, of which 8 were waited for; matrix products, arithmetic and copies ran while one was open for 12% of the time, Pallas kernels for 0%

commit v1 on v0

v1 whole, which is shorter than its diff:
```python
import functools

import jax
import jax.numpy as jnp
from jax import lax
from jax.experimental import pallas as pl
from jax.experimental.pallas import tpu as pltpu
from jax.sharding import PartitionSpec as P

ROUNDS = 3
NEWTON = 4
MESH = pl.DeviceIdType.MESH

FIRST = (
    ((1, 1), (0, 1)),
    ((1, 1), (0, -1), (0, 1)),
    ((0, -1), (1, 1), (1, -1)),
    ((0, -1), (1, -1)),
)
ARRIVE = (
    ((1, 0, 0), (2, 0, 0), (3, 0, 0)),
    ((0, 1, 1), (2, 0, -1), (0, 0, 1), (2, 1, 0), (3, 0, -1), (3, 1, 0)),
    ((3, 0, -1), (1, 1, 1), (3, 1, -1), (1, 0, 0), (0, 1, 1), (0, 0, 0)),
    ((2, 1, 0), (1, 1, 0), (0, 1, 0)),
)


def pair_minor(upper, lower, left, right):
    return upper[left] * lower[right] - upper[right] * lower[left]


def deviation(m, total):
    keyed = [
        [m[0][0] + m[1][1] + m[2][2], m[1][2] - m[2][1], m[2][0] - m[0][2], m[0][1] - m[1][0]],
        [m[1][2] - m[2][1], m[0][0] - m[1][1] - m[2][2], m[0][1] + m[1][0], m[2][0] + m[0][2]],
        [m[2][0] - m[0][2], m[0][1] + m[1][0], -m[0][0] + m[1][1] - m[2][2], m[1][2] + m[2][1]],
        [m[0][1] - m[1][0], m[2][0] + m[0][2], m[1][2] + m[2][1], -m[0][0] - m[1][1] + m[2][2]],
    ]
    top_one, top_two, low_one, low_two = keyed
    det_key = (
        pair_minor(top_one, top_two, 0, 1) * pair_minor(low_one, low_two, 2, 3)
        - pair_minor(top_one, top_two, 0, 2) * pair_minor(low_one, low_two, 1, 3)
        + pair_minor(top_one, top_two, 0, 3) * pair_minor(low_one, low_two, 1, 2)
        + pair_minor(top_one, top_two, 1, 2) * pair_minor(low_one, low_two, 0, 3)
        - pair_minor(top_one, top_two, 1, 3) * pair_minor(low_one, low_two, 0, 2)
        + pair_minor(top_one, top_two, 2, 3) * pair_minor(low_one, low_two, 0, 1)
    )
    det_three = (
        m[0][0] * (m[1][1] * m[2][2] - m[1][2] * m[2][1])
        - m[0][1] * (m[1][0] * m[2][2] - m[1][2] * m[2][0])
        + m[0][2] * (m[1][0] * m[2][1] - m[1][1] * m[2][0])
    )
    square_sum = m[0][0] * m[0][0]
    for first in range(3):
        for second in range(3):
            if first + second > 0:
                square_sum = square_sum + m[first][second] * m[first][second]
    second_coef = -2.0 * square_sum
    first_coef = -8.0 * det_three
    largest = 0.5 * total
    for newton_step in range(NEWTON):
        squared = largest * largest
        polynomial = squared * squared + second_coef * squared + first_coef * largest + det_key
        derivative = 4.0 * squared * largest + 2.0 * second_coef * largest + first_coef
        largest = largest - polynomial / derivative
    return total - 2.0 * largest


def split(value):
    high = value.astype(jnp.bfloat16)
    low = (value - high.astype(jnp.float32)).astype(jnp.bfloat16)
    return high, low


def kernel(n, reps, coords, cnt, behind, ahead, own, part, pcnt, full, fth, ftl, gh, gl, cov,
           fsq, dev, devt, zs, zr, xs, pr, cs, cr, os, br, ar, ls):
    b = lax.axis_index("blk")
    z = lax.axis_index("rep")
    par = lax.rem(b, 2)
    atoms = coords.shape[1]
    half = coords.shape[2] // 2
    quarter = half // 2
    pitch = (atoms + 15) // 16 * 16
    natom = atoms * reps
    fh = z // 2
    gside = lax.rem(z, 2)

    def at(step):
        return lax.rem(b + step + n, n)

    barrier = pltpu.get_barrier_semaphore()
    for step in range(-ROUNDS, ROUNDS + 1):
        for turn in range(reps):
            if step or turn:
                pl.semaphore_signal(barrier, inc=1, device_id=(at(step), lax.rem(z + turn, reps)),
                                    device_id_type=MESH)
    pl.semaphore_wait(barrier, (2 * ROUNDS + 1) * reps - 1)

    def remote(src, dst, send, recv, where):
        return pltpu.make_async_remote_copy(src_ref=src, dst_ref=dst, send_sem=send, recv_sem=recv,
                                            device_id=where, device_id_type=MESH)

    def along(me, s, h, k, step):
        src = coords.at[k, :, pl.ds(h * half, half)] if s == me else own.at[s, h, k]
        return remote(src, own.at[s, h, k], zs.at[(step + 1) // 2, s, h, k], zr.at[s, h, k],
                      (b, z + step))

    def across(me, s, k):
        h = me % 2
        src = coords.at[k, :, pl.ds(h * half, half)] if s == me else own.at[s, h, k]
        slot = 2 * par
        return (
            remote(src, part.at[1, s, k], xs.at[0, s, k], pr.at[1, s, k], (at(2), z)),
            remote(src, part.at[slot, s, k], xs.at[1, s, k], pr.at[slot, s, k], (at(1 + slot), z)),
        )

    def relay(s, k):
        slot = 2 - 2 * par
        return remote(part.at[1, s, k], part.at[slot, s, k], xs.at[2, s, k], pr.at[slot, s, k],
                      (at(1 - 2 * par), z))

    def count_copy(d):
        return remote(cnt, pcnt.at[d], cs.at[d], cr.at[d], (at(d + 1), z))

    def local():
        return pltpu.make_async_copy(coords.at[:, :, pl.ds(pl.multiple_of(fh * half, half), half)],
                                     own.at[z, fh], ls)

    def behind_copy(d):
        other = pl.multiple_of(quarter * (1 - gside), quarter)
        cols = pl.ds(pl.multiple_of(gside * half, half), half)
        return remote(dev.at[d, pl.ds(other, quarter)], behind.at[d, :, cols], os.at[d, 0],
                      br.at[d], (b, z + 1 - 2 * gside))

    def ahead_copy(d, j):
        cols = pl.ds(pl.multiple_of(fh * half, half), half)
        return remote(devt.at[d, pl.ds(j * quarter, quarter)], ahead.at[d, :, cols],
                      os.at[d, 1 + j], ar.at[d, fh], (lax.rem(b - 1 - d + n, n), 2 * gside + j))

    def program(me):
        for h, step in FIRST[me]:
            for k in range(3):
                along(me, me, h, k, step).start()
        for k in range(3):
            for copy in across(me, me, k):
                copy.start()
        local().start()
        for d in range(ROUNDS):
            count_copy(d).start()
        pending = [me]
        for s, h, step in ARRIVE[me]:
            fresh = h == me % 2
            for k in range(3):
                zr_wait(s, h, k)
                if step:
                    along(me, s, h, k, step).start()
                if fresh:
                    for copy in across(me, s, k):
                        copy.start()
            if fresh:
                due = pending.pop(0)
                for k in range(3):
                    pr_wait(1, due, k)
                    relay(due, k).start()
                pending.append(s)
        for due in pending:
            for k in range(3):
                pr_wait(1, due, k)
                relay(due, k).start()

    def zr_wait(s, h, k):
        remote(own.at[s, h, k], own.at[s, h, k], zs.at[0, s, h, k], zr.at[s, h, k],
               (b, lax.rem(z + 1, reps))).wait_recv()

    def pr_wait(d, s, k):
        remote(part.at[d, s, k], part.at[d, s, k], xs.at[0, s, k], pr.at[d, s, k],
               (b, lax.rem(z + 1, reps))).wait_recv()

    def finish(me):
        for h, step in FIRST[me]:
            for k in range(3):
                along(me, me, h, k, step).wait_send()
        for s, h, step in ARRIVE[me]:
            if step:
                for k in range(3):
                    along(me, s, h, k, step).wait_send()
        for s in range(reps):
            for k in range(3):
                for copy in across(me, s, k):
                    copy.wait_send()
                relay(s, k).wait_send()

    for me in range(reps):
        @pl.when(z == me)
        def _(me=me):
            program(me)

    local().wait()
    full[...] = jnp.zeros_like(full)
    gh[...] = jnp.zeros_like(gh)
    gl[...] = jnp.zeros_like(gl)
    fsq[...] = jnp.zeros_like(fsq)
    for k in range(3):
        mean = sum(jnp.sum(own[s, fh, k], axis=0, keepdims=True) for s in range(reps)) / natom
        for s in range(reps):
            full[s * pitch:s * pitch + atoms, :] = own[s, fh, k] - mean
        turned = full[...].T
        fsq[...] += jnp.broadcast_to(jnp.sum(turned * turned, axis=1, keepdims=True), fsq.shape)
        high, low = split(turned)
        fth[k * half:(k + 1) * half, :] = high
        ftl[k * half:(k + 1) * half, :] = low
    fsq[...] = fsq[...] / natom
    for d in range(ROUNDS):
        count_copy(d).wait_recv()

    def block(turn, carry):
        d = lax.rem(turn + 1, ROUNDS)

        @pl.when(d != 1)
        def _():
            for s in range(reps):
                for k in range(3):
                    pr_wait(d, s, k)

        square = jnp.zeros((1, half), jnp.float32)
        for k in range(3):
            mean = sum(jnp.sum(part[d, s, k], axis=0, keepdims=True) for s in range(reps)) / natom
            for s in range(reps):
                centered = part[d, s, k] - mean
                square = square + jnp.sum(centered * centered, axis=0, keepdims=True)
                high, low = split(centered)
                gh[s * pitch:s * pitch + atoms, k * half:(k + 1) * half] = high
                gl[s * pitch:s * pitch + atoms, k * half:(k + 1) * half] = low
        square = square / natom
        product = functools.partial(jnp.dot, preferred_element_type=jnp.float32)
        cov[...] = (product(fth[...], gh[...]) + product(fth[...], gl[...])
                    + product(ftl[...], gh[...])) / natom
        rows = 16

        def chunk(i, inner):
            r = pl.multiple_of(i * rows, rows)
            m = [[cov[pl.ds(k * half + r, rows), l * half:(l + 1) * half] for l in range(3)]
                 for k in range(3)]
            total = fsq[pl.ds(r, rows), :] + square
            frame = fh * half + r + lax.broadcasted_iota(jnp.int32, (rows, half), 0)
            other = gside * half + lax.broadcasted_iota(jnp.int32, (rows, half), 1)
            mask = (frame < cnt[0:1, :]) & (other < pcnt[d, 0:1, :])
            dev[d, pl.ds(r, rows), :] = jnp.where(mask, deviation(m, total), 0.0)
            return inner

        lax.fori_loop(0, half // rows, chunk, 0)
        behind_copy(d).start()
        devt[d] = dev[d].T
        cols = pl.ds(pl.multiple_of(gside * half, half), half)
        behind[d, :, cols] = dev[d, pl.ds(pl.multiple_of(quarter * gside, quarter), quarter), :]
        for j in range(2):
            ahead_copy(d, j).start()
        return carry

    lax.fori_loop(0, ROUNDS, block, 0)
    for me in range(reps):
        @pl.when(z == me)
        def _(me=me):
            finish(me)
    for d in range(ROUNDS):
        count_copy(d).wait_send()
        behind_copy(d).wait()
        for j in range(2):
            ahead_copy(d, j).wait_send()
            remote(devt.at[d, pl.ds(0, quarter)], ahead.at[d, :, pl.ds(j * half, half)],
                   os.at[d, 1], ar.at[d, j], (at(1), z)).wait_recv()


def shards(n, reps, coords, frame_count):
    atoms, frames = coords.shape[1], coords.shape[2]
    half = frames // 2
    depth = ((atoms + 15) // 16 * 16 * reps + 127) // 128 * 128
    counts = jnp.broadcast_to(frame_count.astype(jnp.int32)[:, None], (8, half))
    f32, bf16 = jnp.float32, jnp.bfloat16
    dma = pltpu.SemaphoreType.DMA
    vmem = pl.BlockSpec(memory_space=pltpu.VMEM)
    result = jax.ShapeDtypeStruct((ROUNDS, frames // reps, frames), f32)
    return pl.pallas_call(
        functools.partial(kernel, n, reps),
        out_shape=(result, result),
        in_specs=[pl.BlockSpec(memory_space=pl.ANY), vmem],
        out_specs=(vmem, vmem),
        scratch_shapes=[
            pltpu.VMEM((reps, 2, 3, atoms, half), f32),
            pltpu.VMEM((ROUNDS, reps, 3, atoms, half), f32),
            pltpu.VMEM((ROUNDS, 8, half), jnp.int32),
            pltpu.VMEM((depth, half), f32),
            pltpu.VMEM((3 * half, depth), bf16),
            pltpu.VMEM((3 * half, depth), bf16),
            pltpu.VMEM((depth, 3 * half), bf16),
            pltpu.VMEM((depth, 3 * half), bf16),
            pltpu.VMEM((3 * half, 3 * half), f32),
            pltpu.VMEM((half, half), f32),
            pltpu.VMEM((ROUNDS, half, half), f32),
            pltpu.VMEM((ROUNDS, half, half), f32),
            dma((2, reps, 2, 3)),
            dma((reps, 2, 3)),
            dma((3, reps, 3)),
            dma((ROUNDS, reps, 3)),
            dma((ROUNDS,)),
            dma((ROUNDS,)),
            dma((ROUNDS, 3)),
            dma((ROUNDS,)),
            dma((ROUNDS, 2)),
            dma(()),
        ],
        compiler_params=pltpu.CompilerParams(collective_id=0, has_side_effects=True),
    )(coords, counts)


def solution(mesh):
    in_specs = (P(None, "rep", "blk"), P("blk"))
    out_specs = (P(None, ("blk", "rep"), None), P(None, ("blk", "rep"), None))
    body = functools.partial(shards, mesh.shape["blk"], mesh.shape["rep"])
    return jax.shard_map(body, mesh=mesh, in_specs=in_specs, out_specs=out_specs, check_vma=False)
```

time: 229 us -> 84 us (0.37)
  waiting for transfers between devices: 112 us -> 0 us
  Pallas kernels: 0 us -> 79.6 us
  starting transfers between devices: 41 us -> 0 us
  blocking collectives: 22.3 us -> 0 us
  other arithmetic: 14.9 us -> 0 us
  between operations: 15 us -> 1.29 us
  matrix products: 12.4 us -> 0 us
  local copies, waits for them, and re-layouts: 10.9 us -> 2.93 us
    all_gather x1 -> x0, waiting for transfers between devices: 91 us -> none  [shards(): whole_atoms = lax.all_gather(centered, 'rep', axis=1, tiled=True)]
    pallas_call x0 -> x1, Pallas kernels: none -> 79.6 us  [shards(): pl.pallas_call(functools.partial(kernel, n, reps), out_shape=(result, res...]
    ppermute x12 -> x0, starting transfers between devices: 31.1 us -> none  [from_behind(): return lax.ppermute(block, axis, route)]
    psum x2 -> x0, blocking collectives: 22.3 us -> none  [the longest x1 13.5 us: shards(): atom_sums = lax.psum(jnp.sum(coords, axis=1), 'rep')]
    ppermute x12 -> x0, waiting for transfers between devices: 12.5 us -> none  [from_behind(): return lax.ppermute(block, axis, route)]
    dot_general x3 -> x0, matrix products: 12.4 us -> none  [shards(): lax.dot_general(whole_atoms, partner_coords, (((1,), (1,)), ((), ())), pr...]
    all_to_all x3 -> x0, starting transfers between devices: 9.86 us -> none  [shards(): lax.all_to_all(square, 'rep', split_axis=0, concat_axis=1, tiled=True)]
    all_to_all x3 -> x0, waiting for transfers between devices: 8.13 us -> none  [shards(): lax.all_to_all(square, 'rep', split_axis=0, concat_axis=1, tiled=True)]
  transfers between devices with their start and end apart: 16 -> 0, of which waited for: 8 -> 0; matrix products, arithmetic and copies ran while one was open for 12% -> 0% of each run, Pallas kernels for 0% -> 0%
where the time goes in v1:
time: 84 us; the launch traced here: 83.8 us
  Pallas kernels  79.6 us (95%)
  local copies, waits for them, and re-layouts  2.93 us (3%)
  between operations  1.29 us (2%)
    pallas_call x1, Pallas kernels, shards(): pl.pallas_call(functools.partial(kernel, n, reps), out_shape=(result, res...  79.6 us
    unnamed x4, local copies, waits for them, and re-layouts  2.34 us

profile of v1, /device:TPU:0, one launch (start us, length us, event | category | flops | bytes accessed | tf_op | source)
XLA Modules:
  0.0 83.8 jit_solution(12486319629439192393)
XLA Ops:
  1.3 0.6 broadcast_in_dim.9.cnt
  1.9 79.6 %shard_map.41 = (f32[3,64,256]{2,1,0:T(8,128)}, f32[3,64,256]{2,1,0:T(8,128)}) custom-call(f32[3,300,256]{2,1,0:T(8,128)} %coords.1, s32[8,128]{1,0:T(8,128)} %broadcast_in_dim.9.cnt), custom_call_target="tpu_custom_call" | custom-call | tf_op jit(solution)/shard_map/pallas_call | solution.py:283
  81.4 0.0 copy-start
  81.4 1.7 %copy.7 = f32[3,64,256]{2,1,0:T(8,128)} copy(f32[3,64,256]{2,1,0:T(8,128)} %get-tuple-element.4) | data formatting | bytes 393216
  83.1 0.0 copy-done
  83.1 0.7 copy.8
Async XLA Ops:
  81.4 1.7 %copy-start = (f32[3,64,256]{2,1,0:T(8,128)S(1)}, f32[3,64,256]{2,1,0:T(8,128)}, u32[]{:S(2)}) copy-start(f32[3,64,256]{2,1,0:T(8,128)} %get-tuple-element.5) | copy-start | bytes 589828

commit v2 on v1

--- a/solution.py
+++ b/solution.py
@@ -11,18 +11,21 @@
 NEWTON = 4
 MESH = pl.DeviceIdType.MESH
 
+ALL = (0, 1, 2)
 FIRST = (
-    ((1, 1), (0, 1)),
-    ((1, 1), (0, -1), (0, 1)),
-    ((0, -1), (1, 1), (1, -1)),
-    ((0, -1), (1, -1)),
+    ((1, 1, ALL), (0, 1, ALL)),
+    ((1, 1, ALL), (0, -1, ALL), (0, 1, (0,))),
+    ((0, -1, ALL), (1, 1, ALL), (1, -1, (0,))),
+    ((0, -1, ALL), (1, -1, ALL)),
 )
+LATE = ((), ((0, 1, (1, 2)),), ((1, -1, (1, 2)),), ())
 ARRIVE = (
-    ((1, 0, 0), (2, 0, 0), (3, 0, 0)),
-    ((0, 1, 1), (2, 0, -1), (0, 0, 1), (2, 1, 0), (3, 0, -1), (3, 1, 0)),
-    ((3, 0, -1), (1, 1, 1), (3, 1, -1), (1, 0, 0), (0, 1, 1), (0, 0, 0)),
-    ((2, 1, 0), (1, 1, 0), (0, 1, 0)),
+    (((1, 0, 0),), ((2, 0, 0),), ((3, 0, 0),)),
+    (((2, 0, -1), (0, 1, 1)), ((3, 0, -1), (0, 0, 1))),
+    (((1, 1, 1), (3, 0, -1)), ((0, 1, 1), (3, 1, -1))),
+    (((2, 1, 0),), ((1, 1, 0),), ((0, 1, 0),)),
 )
+LAST = ((), ((2, 1), (3, 1)), ((1, 0), (0, 0)), ())
 
 
 def pair_minor(upper, lower, left, right):
@@ -77,24 +80,34 @@
     b = lax.axis_index("blk")
     z = lax.axis_index("rep")
     par = lax.rem(b, 2)
+    bent = lax.rem(b // 2, 2) * par == 1
+    bends = lax.rem(b // 2, 2) * (1 - par) == 1
     atoms = coords.shape[1]
     half = coords.shape[2] // 2
     quarter = half // 2
     pitch = (atoms + 15) // 16 * 16
     natom = atoms * reps
-    fh = z // 2
-    gside = lax.rem(z, 2)
+    fh = lax.rem(z, 2)
+    gside = z // 2
 
     def at(step):
         return lax.rem(b + step + n, n)
 
     barrier = pltpu.get_barrier_semaphore()
     for step in range(-ROUNDS, ROUNDS + 1):
-        for turn in range(reps):
-            if step or turn:
-                pl.semaphore_signal(barrier, inc=1, device_id=(at(step), lax.rem(z + turn, reps)),
-                                    device_id_type=MESH)
-    pl.semaphore_wait(barrier, (2 * ROUNDS + 1) * reps - 1)
+        if step:
+            pl.semaphore_signal(barrier, inc=1, device_id=(at(step), z), device_id_type=MESH)
+
+    @pl.when(z > 0)
+    def _():
+        pl.semaphore_signal(barrier, inc=1, device_id=(b, z - 1), device_id_type=MESH)
+
+    @pl.when(z < reps - 1)
+    def _():
+        pl.semaphore_signal(barrier, inc=1, device_id=(b, z + 1), device_id_type=MESH)
+
+    inner = jnp.minimum(z, 1) * jnp.minimum(reps - 1 - z, 1)
+    pl.semaphore_wait(barrier, 2 * ROUNDS + 1 + inner)
 
     def remote(src, dst, send, recv, where):
         return pltpu.make_async_remote_copy(src_ref=src, dst_ref=dst, send_sem=send, recv_sem=recv,
@@ -106,19 +119,42 @@
                       (b, z + step))
 
     def across(me, s, k):
-        h = me % 2
+        h = me // 2
         src = coords.at[k, :, pl.ds(h * half, half)] if s == me else own.at[s, h, k]
         slot = 2 * par
         return (
+            remote(src, part.at[slot, s, k], xs.at[1, s, k], pr.at[slot, s, k], (at(1 + slot), z)),
             remote(src, part.at[1, s, k], xs.at[0, s, k], pr.at[1, s, k], (at(2), z)),
-            remote(src, part.at[slot, s, k], xs.at[1, s, k], pr.at[slot, s, k], (at(1 + slot), z)),
         )
+
+    def across_start(me, s, k):
+        first, second = across(me, s, k)
+        first.start()
+
+        @pl.when(jnp.logical_not(bent))
+        def _():
+            second.start()
+
+    def bend(s, k):
+        return remote(part.at[2, s, k], part.at[1, s, k], xs.at[3, s, k], pr.at[1, s, k],
+                      (at(-1), z))
 
     def relay(s, k):
         slot = 2 - 2 * par
         return remote(part.at[1, s, k], part.at[slot, s, k], xs.at[2, s, k], pr.at[slot, s, k],
                       (at(1 - 2 * par), z))
 
+    def pass_on(s):
+        @pl.when(bends)
+        def _():
+            for k in range(3):
+                pr_wait(2, s, k)
+                bend(s, k).start()
+
+        for k in range(3):
+            pr_wait(1, s, k)
+            relay(s, k).start()
+
     def count_copy(d):
         return remote(cnt, pcnt.at[d], cs.at[d], cr.at[d], (at(d + 1), z))
 
@@ -126,47 +162,46 @@
         return pltpu.make_async_copy(coords.at[:, :, pl.ds(pl.multiple_of(fh * half, half), half)],
                                      own.at[z, fh], ls)
 
-    def behind_copy(d):
-        other = pl.multiple_of(quarter * (1 - gside), quarter)
-        cols = pl.ds(pl.multiple_of(gside * half, half), half)
-        return remote(dev.at[d, pl.ds(other, quarter)], behind.at[d, :, cols], os.at[d, 0],
-                      br.at[d], (b, z + 1 - 2 * gside))
+    cols = pl.ds(pl.multiple_of(gside * half, half), half)
+
+    def behind_copy(d, j):
+        return remote(dev.at[d, pl.ds(j * quarter, quarter)], behind.at[d, :, cols],
+                      os.at[d, 2 + j], br.at[d, gside], (b, 2 * fh + j))
 
     def ahead_copy(d, j):
-        cols = pl.ds(pl.multiple_of(fh * half, half), half)
-        return remote(devt.at[d, pl.ds(j * quarter, quarter)], ahead.at[d, :, cols],
-                      os.at[d, 1 + j], ar.at[d, fh], (lax.rem(b - 1 - d + n, n), 2 * gside + j))
+        mine = pl.ds(pl.multiple_of(fh * half, half), half)
+        return remote(devt.at[d, pl.ds(j * quarter, quarter)], ahead.at[d, :, mine],
+                      os.at[d, j], ar.at[d, fh], (lax.rem(b - 1 - d + n, n), 2 * gside + j))
 
     def program(me):
-        for h, step in FIRST[me]:
-            for k in range(3):
+        for h, step, parts in FIRST[me]:
+            for k in parts:
                 along(me, me, h, k, step).start()
         for k in range(3):
-            for copy in across(me, me, k):
-                copy.start()
+            across_start(me, me, k)
         local().start()
         for d in range(ROUNDS):
             count_copy(d).start()
         pending = [me]
-        for s, h, step in ARRIVE[me]:
-            fresh = h == me % 2
+        for turn, group in enumerate(ARRIVE[me]):
+            for k in range(3):
+                for s, h, step in group:
+                    zr_wait(s, h, k)
+                    if step:
+                        along(me, s, h, k, step).start()
+                    if h == me // 2:
+                        across_start(me, s, k)
+            if turn == 0:
+                for h, step, parts in LATE[me]:
+                    for k in parts:
+                        along(me, me, h, k, step).start()
+            pass_on(pending.pop(0))
+            pending.extend(s for s, h, step in group if h == me // 2)
+        for due in pending:
+            pass_on(due)
+        for s, h in LAST[me]:
             for k in range(3):
                 zr_wait(s, h, k)
-                if step:
-                    along(me, s, h, k, step).start()
-                if fresh:
-                    for copy in across(me, s, k):
-                        copy.start()
-            if fresh:
-                due = pending.pop(0)
-                for k in range(3):
-                    pr_wait(1, due, k)
-                    relay(due, k).start()
-                pending.append(s)
-        for due in pending:
-            for k in range(3):
-                pr_wait(1, due, k)
-                relay(due, k).start()
 
     def zr_wait(s, h, k):
         remote(own.at[s, h, k], own.at[s, h, k], zs.at[0, s, h, k], zr.at[s, h, k],
@@ -177,18 +212,27 @@
                (b, lax.rem(z + 1, reps))).wait_recv()
 
     def finish(me):
-        for h, step in FIRST[me]:
-            for k in range(3):
+        for h, step, parts in FIRST[me] + LATE[me]:
+            for k in parts:
                 along(me, me, h, k, step).wait_send()
-        for s, h, step in ARRIVE[me]:
-            if step:
-                for k in range(3):
-                    along(me, s, h, k, step).wait_send()
+        for group in ARRIVE[me]:
+            for s, h, step in group:
+                if step:
+                    for k in range(3):
+                        along(me, s, h, k, step).wait_send()
         for s in range(reps):
             for k in range(3):
-                for copy in across(me, s, k):
-                    copy.wait_send()
+                first, second = across(me, s, k)
+                first.wait_send()
                 relay(s, k).wait_send()
+
+                @pl.when(jnp.logical_not(bent))
+                def _(second=second):
+                    second.wait_send()
+
+                @pl.when(bends)
+                def _(s=s, k=k):
+                    bend(s, k).wait_send()
 
     for me in range(reps):
         @pl.when(z == me)
@@ -216,7 +260,7 @@
     def block(turn, carry):
         d = lax.rem(turn + 1, ROUNDS)
 
-        @pl.when(d != 1)
+        @pl.when((d == 0) | ((d == 2) & jnp.logical_not(bends)))
         def _():
             for s in range(reps):
                 for k in range(3):
@@ -249,12 +293,17 @@
             return inner
 
         lax.fori_loop(0, half // rows, chunk, 0)
-        behind_copy(d).start()
         devt[d] = dev[d].T
-        cols = pl.ds(pl.multiple_of(gside * half, half), half)
-        behind[d, :, cols] = dev[d, pl.ds(pl.multiple_of(quarter * gside, quarter), quarter), :]
         for j in range(2):
             ahead_copy(d, j).start()
+
+            @pl.when(z != 2 * fh + j)
+            def _(j=j):
+                behind_copy(d, j).start()
+
+            @pl.when(z == 2 * fh + j)
+            def _(j=j):
+                behind[d, :, cols] = dev[d, j * quarter:(j + 1) * quarter, :]
         return carry
 
     lax.fori_loop(0, ROUNDS, block, 0)
@@ -264,11 +313,20 @@
             finish(me)
     for d in range(ROUNDS):
         count_copy(d).wait_send()
-        behind_copy(d).wait()
         for j in range(2):
             ahead_copy(d, j).wait_send()
+
+            @pl.when(z != 2 * fh + j)
+            def _(d=d, j=j):
+                behind_copy(d, j).wait_send()
+
+            @pl.when(z != z // 2 + 2 * j)
+            def _(d=d, j=j):
+                remote(dev.at[d, pl.ds(0, quarter)], behind.at[d, :, pl.ds(j * half, half)],
+                       os.at[d, 2], br.at[d, j], (at(1), z)).wait_recv()
+
             remote(devt.at[d, pl.ds(0, quarter)], ahead.at[d, :, pl.ds(j * half, half)],
-                   os.at[d, 1], ar.at[d, j], (at(1), z)).wait_recv()
+                   os.at[d, 0], ar.at[d, j], (at(1), z)).wait_recv()
 
 
 def shards(n, reps, coords, frame_count):
@@ -300,12 +358,12 @@
             pltpu.VMEM((ROUNDS, half, half), f32),
             dma((2, reps, 2, 3)),
             dma((reps, 2, 3)),
-            dma((3, reps, 3)),
+            dma((4, reps, 3)),
             dma((ROUNDS, reps, 3)),
             dma((ROUNDS,)),
             dma((ROUNDS,)),
-            dma((ROUNDS, 3)),
-            dma((ROUNDS,)),
+            dma((ROUNDS, 4)),
+            dma((ROUNDS, 2)),
             dma((ROUNDS, 2)),
             dma(()),
         ],

time: 84 us -> 70.6 us (0.84)
  Pallas kernels: 79.6 us -> 66.2 us
    pallas_call x1, Pallas kernels: 79.6 us -> 66.2 us  [shards(): pl.pallas_call(functools.partial(kernel, n, reps), out_shape=(result, res...]
where the time goes in v2:
time: 70.6 us; the launch traced here: 70.4 us
  Pallas kernels  66.2 us (94%)
  local copies, waits for them, and re-layouts  2.93 us (4%)
  between operations  1.29 us (2%)
    pallas_call x1, Pallas kernels, shards(): pl.pallas_call(functools.partial(kernel, n, reps), out_shape=(result, res...  66.2 us
    unnamed x4, local copies, waits for them, and re-layouts  2.34 us

profile of v2, /device:TPU:0, one launch (start us, length us, event | category | flops | bytes accessed | tf_op | source)
XLA Modules:
  0.0 70.4 jit_solution(10392801551778464128)
XLA Ops:
  1.3 0.6 broadcast_in_dim.9.cnt
  1.9 66.2 %shard_map.41 = (f32[3,64,256]{2,1,0:T(8,128)}, f32[3,64,256]{2,1,0:T(8,128)}) custom-call(f32[3,300,256]{2,1,0:T(8,128)} %coords.1, s32[8,128]{1,0:T(8,128)} %broadcast_in_dim.9.cnt), custom_call_target="tpu_custom_call" | custom-call | tf_op jit(solution)/shard_map/pallas_call | solution.py:341
  68.1 0.0 copy-start
  68.1 1.7 %copy.7 = f32[3,64,256]{2,1,0:T(8,128)} copy(f32[3,64,256]{2,1,0:T(8,128)} %get-tuple-element.4) | data formatting | bytes 393216
  69.8 0.0 copy-done
  69.8 0.7 copy.8
Async XLA Ops:
  68.1 1.7 %copy-start = (f32[3,64,256]{2,1,0:T(8,128)S(1)}, f32[3,64,256]{2,1,0:T(8,128)}, u32[]{:S(2)}) copy-start(f32[3,64,256]{2,1,0:T(8,128)} %get-tuple-element.5) | copy-start | bytes 589828

commit v3 on v2

--- a/solution.py
+++ b/solution.py
@@ -144,16 +144,17 @@
         return remote(part.at[1, s, k], part.at[slot, s, k], xs.at[2, s, k], pr.at[slot, s, k],
                       (at(1 - 2 * par), z))
 
-    def pass_on(s):
-        @pl.when(bends)
-        def _():
-            for k in range(3):
-                pr_wait(2, s, k)
-                bend(s, k).start()
-
+    def pass_on(*sources):
         for k in range(3):
-            pr_wait(1, s, k)
-            relay(s, k).start()
+            @pl.when(bends)
+            def _(k=k):
+                for s in sources:
+                    pr_wait(2, s, k)
+                    bend(s, k).start()
+
+            for s in sources:
+                pr_wait(1, s, k)
+                relay(s, k).start()
 
     def count_copy(d):
         return remote(cnt, pcnt.at[d], cs.at[d], cr.at[d], (at(d + 1), z))
@@ -197,8 +198,7 @@
                         along(me, me, h, k, step).start()
             pass_on(pending.pop(0))
             pending.extend(s for s, h, step in group if h == me // 2)
-        for due in pending:
-            pass_on(due)
+        pass_on(*pending)
         for s, h in LAST[me]:
             for k in range(3):
                 zr_wait(s, h, k)

time: 70.6 us -> 70.6 us (level)
  no operation moved by 1% of the time
where the time goes in v3:
time: 70.6 us; the launch traced here: 70.4 us
  Pallas kernels  66.2 us (94%)
  local copies, waits for them, and re-layouts  2.93 us (4%)
  between operations  1.29 us (2%)
    pallas_call x1, Pallas kernels, shards(): pl.pallas_call(functools.partial(kernel, n, reps), out_shape=(result, res...  66.2 us
    unnamed x4, local copies, waits for them, and re-layouts  2.34 us

profile of v3, /device:TPU:0, one launch (start us, length us, event | category | flops | bytes accessed | tf_op | source)
XLA Modules:
  0.0 70.4 jit_solution(8085218798831182144)
XLA Ops:
  1.3 0.6 broadcast_in_dim.9.cnt
  1.9 66.2 %shard_map.41 = (f32[3,64,256]{2,1,0:T(8,128)}, f32[3,64,256]{2,1,0:T(8,128)}) custom-call(f32[3,300,256]{2,1,0:T(8,128)} %coords.1, s32[8,128]{1,0:T(8,128)} %broadcast_in_dim.9.cnt), custom_call_target="tpu_custom_call" | custom-call | tf_op jit(solution)/shard_map/pallas_call | solution.py:341
  68.1 0.0 copy-start
  68.1 1.7 %copy.7 = f32[3,64,256]{2,1,0:T(8,128)} copy(f32[3,64,256]{2,1,0:T(8,128)} %get-tuple-element.4) | data formatting | bytes 393216
  69.8 0.0 copy-done
  69.8 0.7 copy.8
Async XLA Ops:
  68.1 1.7 %copy-start = (f32[3,64,256]{2,1,0:T(8,128)S(1)}, f32[3,64,256]{2,1,0:T(8,128)}, u32[]{:S(2)}) copy-start(f32[3,64,256]{2,1,0:T(8,128)} %get-tuple-element.5) | copy-start | bytes 589828

commit v4 on v3

--- a/solution.py
+++ b/solution.py
@@ -279,7 +279,7 @@
         product = functools.partial(jnp.dot, preferred_element_type=jnp.float32)
         cov[...] = (product(fth[...], gh[...]) + product(fth[...], gl[...])
                     + product(ftl[...], gh[...])) / natom
-        rows = 16
+        rows = half // 4
 
         def chunk(i, inner):
             r = pl.multiple_of(i * rows, rows)

time: 70.6 us -> 70.2 us (level)
  no operation moved by 1% of the time
where the time goes in v4:
time: 70.2 us; the launch traced here: 70 us
  Pallas kernels  65.8 us (94%)
  local copies, waits for them, and re-layouts  2.93 us (4%)
  between operations  1.29 us (2%)
    pallas_call x1, Pallas kernels, shards(): pl.pallas_call(functools.partial(kernel, n, reps), out_shape=(result, res...  65.8 us
    unnamed x4, local copies, waits for them, and re-layouts  2.34 us

profile of v4, /device:TPU:0, one launch (start us, length us, event | category | flops | bytes accessed | tf_op | source)
XLA Modules:
  0.0 70.0 jit_solution(13468420030389254466)
XLA Ops:
  1.3 0.6 broadcast_in_dim.9.cnt
  1.9 65.8 %shard_map.41 = (f32[3,64,256]{2,1,0:T(8,128)}, f32[3,64,256]{2,1,0:T(8,128)}) custom-call(f32[3,300,256]{2,1,0:T(8,128)} %coords.1, s32[8,128]{1,0:T(8,128)} %broadcast_in_dim.9.cnt), custom_call_target="tpu_custom_call" | custom-call | tf_op jit(solution)/shard_map/pallas_call | solution.py:341
  67.7 0.0 copy-start
  67.7 1.7 %copy.7 = f32[3,64,256]{2,1,0:T(8,128)} copy(f32[3,64,256]{2,1,0:T(8,128)} %get-tuple-element.4) | data formatting | bytes 393216
  69.3 0.0 copy-done
  69.3 0.7 copy.8
Async XLA Ops:
  67.7 1.7 %copy-start = (f32[3,64,256]{2,1,0:T(8,128)S(1)}, f32[3,64,256]{2,1,0:T(8,128)}, u32[]{:S(2)}) copy-start(f32[3,64,256]{2,1,0:T(8,128)} %get-tuple-element.5) | copy-start | bytes 589828
